TPU v7x, 128 devices: a whole 4x4x4 slice. The times are simulated.
128 devices in a mesh: row: 8 (over y, x_lo), col: 16 (over x_hi, z, core).
Axes of the slice: x: 4 (x_hi: 2, x_lo: 2; x = x_hi * 2 + x_lo), y: 4, z: 4, core: 2. Of those that a mesh axis runs over, the one named last changes fastest.
Arguments:
- activations: bfloat16 [2048, 8192], P('col', 'row'), may hold values from -6 to 6
- output_grad: bfloat16 [2048, 8192], P('col', 'row'), may hold values from -1.5 to 1.5
- tile_counts: int32 [32], replicated, may hold values from 16 to 64, as said below
- w_gate: bfloat16 [8192, 15360], P('row', 'col'), may hold values from -0.0625 to 0.0625
- w_up: bfloat16 [8192, 15360], P('row', 'col'), may hold values from -0.0625 to 0.0625
- w_down: bfloat16 [15360, 8192], P('col', 'row'), may hold values from -0.046875 to 0.046875
Outputs:
- input_grad: bfloat16 [2048, 8192], P('col', 'row')
- grad_gate: bfloat16 [8192, 15360], P('row', 'col')
- grad_up: bfloat16 [8192, 15360], P('row', 'col')
- grad_down: bfloat16 [15360, 8192], P('col', 'row')
Inputs may be any that keep to these rules, and one draw needn't show every extreme that they name: `tile_counts`: number of live tokens at the start of each tile of 64 positions; some tile is full and some holds 16.
All inputs are finite; a program needn't handle non-finite values.
Results may differ from a plain program's by a relative error of at most 0.03.
Values may be sent and summed in bfloat16 or wider, within the bound.
No kernel may reach another device: no remote copies, remote signals or barrier semaphores. Data moves between devices by JAX's collectives and lax.ppermute only.
A program may use at most 128 MiB of HBM per device.

v0:
```python
import jax
import jax.numpy as jnp
from jax import lax
from jax.sharding import PartitionSpec as P

TILE = 64


def contract_rows(left, right):
    return lax.dot_general(
        left, right, (((0,), (0,)), ((), ())), preferred_element_type=jnp.float32
    )


def contract_cols(left, right):
    return lax.dot_general(
        left, right, (((1,), (1,)), ((), ())), preferred_element_type=jnp.float32
    )


def swiglu_back(totals, columns):
    gate_sum = totals[:, :columns]
    up_sum = totals[:, columns : 2 * columns]
    back_sum = totals[:, 2 * columns :]
    sigmoid_gate = jax.nn.sigmoid(gate_sum)
    hidden = (gate_sum * sigmoid_gate * up_sum).astype(jnp.bfloat16)
    d_gate = (back_sum * up_sum * sigmoid_gate * (1.0 + gate_sum * (1.0 - sigmoid_gate))).astype(
        jnp.bfloat16
    )
    d_up = (back_sum * gate_sum * sigmoid_gate).astype(jnp.bfloat16)
    return (hidden, d_gate, d_up)


def shards(activations, output_grad, tile_counts, w_gate, w_up, w_down):
    own_rows = activations.shape[0]
    columns = w_gate.shape[1]
    tile_total = tile_counts.shape[0]
    position = lax.axis_index("col") * own_rows + lax.iota(jnp.int32, own_rows)
    in_tile = (position // TILE)[:, None] == lax.iota(jnp.int32, tile_total)[None, :]
    row_limit = jnp.sum(jnp.where(in_tile, tile_counts[None, :], 0), axis=1)
    kept_rows = position % TILE < row_limit
    live_grad = jnp.where(kept_rows[:, None], output_grad, jnp.zeros_like(output_grad))
    inputs_all, grads_all = (
        lax.all_gather(activations, "col", axis=0, tiled=True),
        lax.all_gather(live_grad, "col", axis=0, tiled=True),
    )
    gate_part = jnp.dot(inputs_all, w_gate, preferred_element_type=jnp.float32)
    up_part = jnp.dot(inputs_all, w_up, preferred_element_type=jnp.float32)
    back_part = contract_cols(grads_all, w_down)
    totals = lax.psum_scatter(
        jnp.concatenate([gate_part, up_part, back_part], axis=1).astype(jnp.bfloat16),
        "row",
        scatter_dimension=0,
        tiled=True,
    ).astype(jnp.float32)
    hidden_share, gate_share, up_share = swiglu_back(totals, columns)
    hidden, d_gate, d_up = (
        lax.all_gather(hidden_share, "row", axis=0, tiled=True),
        lax.all_gather(gate_share, "row", axis=0, tiled=True),
        lax.all_gather(up_share, "row", axis=0, tiled=True),
    )
    grad_gate = contract_rows(inputs_all, d_gate).astype(jnp.bfloat16)
    grad_up = contract_rows(inputs_all, d_up).astype(jnp.bfloat16)
    grad_down = contract_rows(hidden, grads_all).astype(jnp.bfloat16)
    input_grad = lax.psum_scatter(
        (contract_cols(d_gate, w_gate) + contract_cols(d_up, w_up)).astype(jnp.bfloat16),
        "col",
        scatter_dimension=0,
        tiled=True,
    )
    return (input_grad, grad_gate, grad_up, grad_down)


def solution(mesh):
    in_specs = (
        P("col", "row"),
        P("col", "row"),
        P(),
        P("row", "col"),
        P("row", "col"),
        P("col", "row"),
    )
    out_specs = (P("col", "row"), P("row", "col"), P("row", "col"), P("col", "row"))
    return jax.shard_map(shards, mesh=mesh, in_specs=in_specs, out_specs=out_specs, check_vma=False)
```

profile of v0, /device:TPU:0, one launch (start us, length us, event | category | flops | bytes accessed | tf_op | source)
XLA Modules:
  0.0 740.1 jit_solution(12108002158446484)
XLA Ops:
  7.2 0.0 all-gather.6.cloned.1.call-start
  7.2 0.7 all-gather.6.cloned.1.call-update
  7.9 0.0 all-gather.8.cloned.1.call-start
  8.0 0.7 select_reduce_fusion
  8.7 1.7 broadcast_select_fusion
  10.5 0.0 reduce-scatter.3.cloned.1.call-start
  10.6 57.9 %all-gather.6.cloned.1.call-done = bf16[2048,1024]{1,0:T(8,128)(2,1)} async-done(((bf16[128,1024]{1,0:T(8,128)(2,1)}), bf16[2048,1024]{1,0:T(8,128)(2,1)}) %all-gather.6.cloned.1.call-update) | async-done | bytes 4194320 | tf_op jit(solution)/shard_map/all_gather | solution.py:44
  68.4 9.1 %convolution_convert_fusion.1 = bf16[2048,960]{0,1:T(8,128)(2,1)} fusion(bf16[2048,1024]{1,0:T(8,128)(2,1)} %all-gather.6.cloned.1.call-done, bf16[1024,960]{0,1:T(8,128)(2,1)} %param.10), kind=kOutput, calls=%fused_computation.3 | convolution fusion | flops 4028497920 | bytes 10092544 | tf_op jit(solution)/shard_map/dot_general | solution.py:48
  77.5 5.9 convolution_convert_fusion.2
  83.4 41.2 %all-gather.8.cloned.1.call-done = bf16[2048,1024]{1,0:T(8,128)(2,1)} async-done(((bf16[128,1024]{1,0:T(8,128)(2,1)}), bf16[2048,1024]{1,0:T(8,128)(2,1)}) %all-gather.8.cloned.1.call-update) | async-done | bytes 4194320 | tf_op jit(solution)/shard_map/all_gather | solution.py:45
  124.7 7.2 convolution_convert_fusion
  131.9 19.8 %pad_maximum_fusion = bf16[2048,2880]{0,1:T(8,128)(2,1)} fusion(bf16[2048,960]{0,1:T(8,128)(2,1)S(1)} %convolution_convert_fusion, bf16[2048,960]{0,1:T(8,128)(2,1)S(1)} %copy-done.2, bf16[2048,960]{0,1:T(8,128)(2,1)S(1)} %copy-done.3), kind=kLoop, calls=%fused_computation | loop fusion | flops 35389440 | bytes 23592960 | tf_op jit(solution)/shard_map/concatenate | solution.py:51
  151.8 0.2 all-gather.10.cloned.1.call-start
  152.0 230.9 %reduce-scatter.3.cloned.1.call-done = bf16[256,2880]{0,1:T(8,128)(2,1)} async-done(((bf16[2048,2880]{0,1:T(8,128)(2,1)}), bf16[256,2880]{0,1:T(8,128)(2,1)}) %reduce-scatter.3.cloned.1.call-update) | async-done | bytes 1474576 | tf_op jit(solution)/shard_map/reduce_scatter | solution.py:50
  382.9 1.6 convert_element_type.31
  384.5 1.7 multiply_convert_fusion
  386.3 0.0 all-gather.10.cloned.1.call-update
  386.3 0.0 all-gather.12.cloned.1.call-start
  386.3 0.5 all-gather.12.cloned.1.call-update
  386.9 0.0 all-gather.14.cloned.1.call-start
  386.9 0.5 all-gather.14.cloned.1.call-update
  387.5 0.0 reduce-scatter.5.cloned.1.call-start
  387.5 84.4 %all-gather.10.cloned.1.call-done = bf16[2048,960]{0,1:T(8,128)(2,1)} async-done(((bf16[256,960]{0,1:T(8,128)(2,1)}), bf16[2048,960]{0,1:T(8,128)(2,1)}) %all-gather.10.cloned.1.call-update) | async-done | bytes 3932176 | tf_op jit(solution)/shard_map/all_gather | solution.py:59
  471.9 8.9 %fusion.1 = f32[2048,1024]{1,0:T(8,128)} fusion(bf16[2048,960]{0,1:T(8,128)(2,1)} %all-gather.10.cloned.1.call-done, bf16[1024,960]{0,1:T(8,128)(2,1)S(1)} %copy-done), kind=kOutput, calls=%fused_computation.22 | convolution fusion | flops 4026531840 | bytes 14286848 | tf_op jit(solution)/shard_map/dot_general | solution.py:16
  480.8 78.6 %all-gather.12.cloned.1.call-done = bf16[2048,960]{0,1:T(8,128)(2,1)} async-done(((bf16[256,960]{0,1:T(8,128)(2,1)}), bf16[2048,960]{0,1:T(8,128)(2,1)}) %all-gather.12.cloned.1.call-update) | async-done | bytes 3932176 | tf_op jit(solution)/shard_map/all_gather | solution.py:60
  559.4 11.6 %add_convert_fusion = bf16[2048,1024]{1,0:T(8,128)(2,1)} fusion(f32[2048,1024]{1,0:T(8,128)} %fusion.1, bf16[2048,960]{0,1:T(8,128)(2,1)} %all-gather.12.cloned.1.call-done, bf16[1024,960]{0,1:T(8,128)(2,1)} %param.10), kind=kOutput, calls=%fused_computation.1 | convolution fusion | flops 4030726144 | bytes 18481152 | tf_op jit(solution)/shard_map/dot_general | solution.py:16
  571.1 0.0 reduce-scatter.5.cloned.1.call-update
  571.1 9.1 %convert_bitcast_fusion = bf16[1024,960]{0,1:T(8,128)(2,1)} fusion(bf16[2048,960]{0,1:T(8,128)(2,1)} %all-gather.12.cloned.1.call-done, bf16[2048,1024]{1,0:T(8,128)(2,1)} %all-gather.6.cloned.1.call-done), kind=kOutput, calls=%fused_computation.5 | convolution fusion | flops 4027514880 | bytes 10092544 | tf_op jit(solution)/shard_map/dot_general | solution.py:10
  580.2 5.4 convert_bitcast_fusion.1
  585.6 61.3 %all-gather.14.cloned.1.call-done = bf16[2048,960]{0,1:T(8,128)(2,1)} async-done(((bf16[256,960]{0,1:T(8,128)(2,1)}), bf16[2048,960]{0,1:T(8,128)(2,1)}) %all-gather.14.cloned.1.call-update) | async-done | bytes 3932176 | tf_op jit(solution)/shard_map/all_gather | solution.py:58
  646.9 9.0 %convolution_convert_fusion.3 = bf16[960,1024]{1,0:T(8,128)(2,1)} fusion(bf16[2048,960]{0,1:T(8,128)(2,1)} %all-gather.14.cloned.1.call-done, bf16[2048,1024]{1,0:T(8,128)(2,1)} %all-gather.8.cloned.1.call-done), kind=kOutput, calls=%fused_computation.7 | convolution fusion | flops 4027514880 | bytes 10092544 | tf_op jit(solution)/shard_map/dot_general | solution.py:10
  655.9 77.3 %reduce-scatter.5.cloned.1.call-done = bf16[128,1024]{1,0:T(8,128)(2,1)} async-done(((bf16[2048,1024]{1,0:T(8,128)(2,1)}), bf16[128,1024]{1,0:T(8,128)(2,1)}) %reduce-scatter.5.cloned.1.call-update) | async-done | bytes 262160 | tf_op jit(solution)/shard_map/reduce_scatter | solution.py:65
  (18 shorter events, 0.1 us)
Async XLA Ops:
  7.2 70.3 %copy-start = (bf16[1024,960]{0,1:T(8,128)(2,1)S(1)}, bf16[1024,960]{0,1:T(8,128)(2,1)}, u32[]{:S(2)}) copy-start(bf16[1024,960]{0,1:T(8,128)(2,1)} %param.9) | copy-start | bytes 5898244
  7.2 61.2 %all-gather.6.cloned.1.call-start = ((), (), s32[]{:S(2)}) async-start(), calls=%async_computation.2 | async-start | bytes 4456448 | tf_op jit(solution)/shard_map/all_gather | solution.py:44
  7.9 116.7 %all-gather.8.cloned.1.call-start = ((), (), s32[]{:S(2)}) async-start(), calls=%async_computation.3 | async-start | bytes 4456448 | tf_op jit(solution)/shard_map/all_gather | solution.py:45
  10.5 372.4 %reduce-scatter.3.cloned.1.call-start = ((), (), s32[]{:S(2)}) async-start(), calls=%async_computation.4 | async-start | bytes 13271040 | tf_op jit(solution)/shard_map/reduce_scatter | solution.py:50
  68.4 9.1 %copy-start.4 = (bf16[2048,1024]{1,0:T(8,128)(2,1)S(1)}, bf16[2048,1024]{1,0:T(8,128)(2,1)}, u32[]{:S(2)}) copy-start(bf16[2048,1024]{1,0:T(8,128)(2,1)} %all-gather.6.cloned.1.call-done) | copy-start | bytes 12582916
  124.7 7.2 copy-start.2
  124.7 7.2 copy-start.3
  151.8 320.1 %all-gather.10.cloned.1.call-start = ((), (), s32[]{:S(2)}) async-start(), calls=%async_computation.5 | async-start | bytes 4423680 | tf_op jit(solution)/shard_map/all_gather | solution.py:59
  386.3 173.1 %all-gather.12.cloned.1.call-start = ((), (), s32[]{:S(2)}) async-start(), calls=%async_computation.6 | async-start | bytes 4423680 | tf_op jit(solution)/shard_map/all_gather | solution.py:60
  386.9 260.0 %all-gather.14.cloned.1.call-start = ((), (), s32[]{:S(2)}) async-start(), calls=%async_computation.8 | async-start | bytes 4423680 | tf_op jit(solution)/shard_map/all_gather | solution.py:58
  387.5 345.8 %reduce-scatter.5.cloned.1.call-start = ((), (), s32[]{:S(2)}) async-start(), calls=%async_computation.7 | async-start | bytes 4456448 | tf_op jit(solution)/shard_map/reduce_scatter | solution.py:65
  571.1 9.1 %copy-start.5 = (bf16[2048,1024]{1,0:T(8,128)(2,1)S(1)}, bf16[2048,1024]{1,0:T(8,128)(2,1)}, u32[]{:S(2)}) copy-start(bf16[2048,1024]{1,0:T(8,128)(2,1)} %all-gather.6.cloned.1.call-done) | copy-start | bytes 12582916
  571.1 9.1 %copy-start.6 = (bf16[2048,960]{0,1:T(8,128)(2,1)S(1)}, bf16[2048,960]{0,1:T(8,128)(2,1)}, u32[]{:S(2)}) copy-start(bf16[2048,960]{0,1:T(8,128)(2,1)} %all-gather.10.cloned.1.call-done) | copy-start | bytes 11796484
  646.9 86.3 %copy-start.1 = (bf16[1024,960]{0,1:T(8,128)(2,1)S(1)}, bf16[1024,960]{0,1:T(8,128)(2,1)}, u32[]{:S(2)}) copy-start(bf16[1024,960]{0,1:T(8,128)(2,1)} %param.9) | copy-start | bytes 5898244
Sparse Core Ops, SparseCore 0:
  10.5 57.8 all-gather.5
  71.5 53.1 all-gather.7
  151.9 230.9 reduce-scatter.2
  386.4 85.4 all-gather.9
  473.9 85.4 all-gather.11
  561.4 85.4 all-gather.13
  651.5 81.6 reduce-scatter.4
where the time goes:
time: 740 us
  waiting for transfers between devices  633 us (86%)
  matrix products  66.3 us (9%)
  other arithmetic  25.7 us (3%)
  between operations  14.2 us (2%)
    reduce_scatter x1, waiting for transfers between devices, shards(): lax.psum_scatter(jnp.concatenate([gate_part, up_part, back_part], axis=1)...  231 us
    all_gather x1, waiting for transfers between devices, shards(): lax.all_gather(gate_share, 'row', axis=0, tiled=True)  84.4 us
    all_gather x1, waiting for transfers between devices, shards(): lax.all_gather(up_share, 'row', axis=0, tiled=True)  78.6 us
    reduce_scatter x1, waiting for transfers between devices, shards(): lax.psum_scatter((contract_cols(d_gate, w_gate) + contract_cols(d_up, w_u...  77.3 us
    all_gather x1, waiting for transfers between devices, shards(): lax.all_gather(hidden_share, 'row', axis=0, tiled=True)  61.3 us
    all_gather x1, waiting for transfers between devices, shards(): lax.all_gather(activations, 'col', axis=0, tiled=True)  57.9 us
    all_gather x1, waiting for transfers between devices, shards(): lax.all_gather(live_grad, 'col', axis=0, tiled=True)  41.2 us
    dot_general x3, matrix products, contract_cols(): lax.dot_general(left, right, (((1,), (1,)), ((), ())), preferred_element_...  27.8 us
  transfers between devices with their start and end apart: 7, of which 7 were waited for; matrix products, arithmetic and copies ran while one was open for 8% of the time, Pallas kernels for 0%

commit v1 on v0

--- a/solution.py
+++ b/solution.py
@@ -56,7 +56,9 @@
     hidden_share, gate_share, up_share = swiglu_back(totals, columns)
     hidden, d_gate, d_up = (
         lax.all_gather(hidden_share, "row", axis=0, tiled=True),
-        lax.all_gather(gate_share, "row", axis=0, tiled=True),
+        jnp.concatenate(
+            lax.all_to_all(jnp.stack([gate_share] * lax.axis_size("row")), "row", 0, 0), axis=0
+        ),
         lax.all_gather(up_share, "row", axis=0, tiled=True),
     )
     grad_gate = contract_rows(inputs_all, d_gate).astype(jnp.bfloat16)

time: 740 us -> 691 us (0.934)
  waiting for transfers between devices: 633 us -> 493 us
  blocking collectives: 0 us -> 91.4 us
    all_to_all x0 -> x1, blocking collectives: none -> 91.4 us  [shards(): lax.all_to_all(jnp.stack([gate_share] * lax.axis_size('row')), 'row', 0, 0)]
    all_gather x1 -> x0, waiting for transfers between devices: 84.4 us -> none  [shards(): lax.all_gather(gate_share, 'row', axis=0, tiled=True)]
    all_gather x1, waiting for transfers between devices: 78.6 us -> 22.6 us  [shards(): lax.all_gather(up_share, 'row', axis=0, tiled=True)]
  transfers between devices with their start and end apart: 7 -> 6, of which waited for: 7 -> 6; matrix products, arithmetic and copies ran while one was open for 8% -> 9% of each run, Pallas kernels for 0% -> 0%
where the time goes in v1:
time: 691 us
  waiting for transfers between devices  493 us (71%)
  blocking collectives  91.4 us (13%)
  matrix products  64.2 us (9%)
  other arithmetic  25.4 us (4%)
  between operations  14.2 us (2%)
    reduce_scatter x1, waiting for transfers between devices, shards(): lax.psum_scatter(jnp.concatenate([gate_part, up_part, back_part], axis=1)...  231 us
    all_to_all x1, blocking collectives, shards(): lax.all_to_all(jnp.stack([gate_share] * lax.axis_size('row')), 'row', 0, 0)  91.4 us
    reduce_scatter x1, waiting for transfers between devices, shards(): lax.psum_scatter((contract_cols(d_gate, w_gate) + contract_cols(d_up, w_u...  77.1 us
    all_gather x1, waiting for transfers between devices, shards(): lax.all_gather(hidden_share, 'row', axis=0, tiled=True)  61.5 us
    all_gather x1, waiting for transfers between devices, shards(): lax.all_gather(activations, 'col', axis=0, tiled=True)  57.9 us
    all_gather x1, waiting for transfers between devices, shards(): lax.all_gather(live_grad, 'col', axis=0, tiled=True)  41.2 us
    dot_general x3, matrix products, contract_cols(): lax.dot_general(left, right, (((1,), (1,)), ((), ())), preferred_element_...  25.7 us
    dot_general x3, matrix products, contract_rows(): lax.dot_general(left, right, (((0,), (0,)), ((), ())), preferred_element_...  23.5 us
  transfers between devices with their start and end apart: 6, of which 6 were waited for; matrix products, arithmetic and copies ran while one was open for 9% of the time, Pallas kernels for 0%

profile of v1, /device:TPU:0, one launch (start us, length us, event | category | flops | bytes accessed | tf_op | source)
XLA Modules:
  0.0 691.0 jit_solution(12483281980457821865)
XLA Ops:
  7.2 0.0 all-gather.5.cloned.1.call-start
  7.2 0.7 all-gather.5.cloned.1.call-update
  7.9 0.0 all-gather.7.cloned.1.call-start
  8.0 0.7 select_reduce_fusion
  8.7 1.7 broadcast_select_fusion
  10.5 0.0 all-gather.7.cloned.1.call-update
  10.5 0.0 reduce-scatter.3.cloned.1.call-start
  10.6 57.9 %all-gather.5.cloned.1.call-done = bf16[2048,1024]{1,0:T(8,128)(2,1)} async-done(((bf16[128,1024]{1,0:T(8,128)(2,1)}), bf16[2048,1024]{1,0:T(8,128)(2,1)}) %all-gather.5.cloned.1.call-update) | async-done | bytes 4194320 | tf_op jit(solution)/shard_map/all_gather | solution.py:44
  68.4 9.1 %convolution_convert_fusion.1 = bf16[2048,960]{0,1:T(8,128)(2,1)} fusion(bf16[2048,1024]{1,0:T(8,128)(2,1)} %all-gather.5.cloned.1.call-done, bf16[1024,960]{0,1:T(8,128)(2,1)} %param.10), kind=kOutput, calls=%fused_computation.3 | convolution fusion | flops 4028497920 | bytes 10092544 | tf_op jit(solution)/shard_map/dot_general | solution.py:48
  77.5 5.9 convolution_convert_fusion.2
  83.4 41.2 %all-gather.7.cloned.1.call-done = bf16[2048,1024]{1,0:T(8,128)(2,1)} async-done(((bf16[128,1024]{1,0:T(8,128)(2,1)}), bf16[2048,1024]{1,0:T(8,128)(2,1)}) %all-gather.7.cloned.1.call-update) | async-done | bytes 4194320 | tf_op jit(solution)/shard_map/all_gather | solution.py:45
  124.7 7.2 %convolution_convert_fusion = bf16[2048,960]{0,1:T(8,128)(2,1)S(1)} fusion(bf16[2048,1024]{1,0:T(8,128)(2,1)} %all-gather.7.cloned.1.call-done, bf16[960,1024]{1,0:T(8,128)(2,1)} %param.11), kind=kOutput, calls=%fused_computation.2 | convolution fusion | flops 4028497920 | bytes 10092544 | tf_op jit(solution)/shard_map/dot_general | solution.py:16
  131.9 19.9 %pad_maximum_fusion = bf16[2048,2880]{0,1:T(8,128)(2,1)} fusion(bf16[2048,960]{0,1:T(8,128)(2,1)S(1)} %convolution_convert_fusion, bf16[2048,960]{0,1:T(8,128)(2,1)S(1)} %copy-done.3, bf16[2048,960]{0,1:T(8,128)(2,1)S(1)} %copy-done.4), kind=kLoop, calls=%fused_computation | loop fusion | flops 35389440 | bytes 23592960 | tf_op jit(solution)/shard_map/concatenate | solution.py:51
  151.8 0.2 all-gather.9.cloned.1.call-start
  152.0 230.9 %reduce-scatter.3.cloned.1.call-done = bf16[256,2880]{0,1:T(8,128)(2,1)} async-done(((bf16[2048,2880]{0,1:T(8,128)(2,1)}), bf16[256,2880]{0,1:T(8,128)(2,1)}) %reduce-scatter.3.cloned.1.call-update) | async-done | bytes 1474576 | tf_op jit(solution)/shard_map/reduce_scatter | solution.py:50
  383.0 1.6 convert_element_type.31
  384.6 1.5 multiply_convert_fusion
  386.1 0.0 all-gather.11.cloned.1.call-start
  386.1 0.5 all-gather.11.cloned.1.call-update
  386.7 0.0 reduce-scatter.5.cloned.1.call-start
  386.7 0.3 stack.2
  387.0 91.4 %all_to_all.5 = bf16[8,256,960]{1,2,0:T(8,128)(2,1)S(1)} all-to-all(bf16[8,256,960]{1,2,0:T(8,128)(2,1)S(1)} %stack.2), channel_id=1, replica_groups=mesh['row'=8,'col'=16] {'row'}, dimensions={0} | all-to-all | bytes 7864320 | tf_op jit(solution)/shard_map/all_to_all | solution.py:60
  478.4 0.5 copy.13
  478.9 1.9 copy-done.2
  480.8 6.8 fusion.1
  487.6 22.6 %all-gather.9.cloned.1.call-done = bf16[2048,960]{0,1:T(8,128)(2,1)} async-done(((bf16[256,960]{0,1:T(8,128)(2,1)}), bf16[2048,960]{0,1:T(8,128)(2,1)}) %all-gather.9.cloned.1.call-update) | async-done | bytes 3932176 | tf_op jit(solution)/shard_map/all_gather | solution.py:62
  510.3 11.6 %add_convert_fusion = bf16[2048,1024]{1,0:T(8,128)(2,1)} fusion(f32[2048,1024]{1,0:T(8,128)} %fusion.1, bf16[2048,960]{0,1:T(8,128)(2,1)} %all-gather.9.cloned.1.call-done, bf16[1024,960]{0,1:T(8,128)(2,1)} %param.10), kind=kOutput, calls=%fused_computation.1 | convolution fusion | flops 4030726144 | bytes 18481152 | tf_op jit(solution)/shard_map/dot_general | solution.py:16
  522.0 9.1 %convert_bitcast_fusion.1 = bf16[1024,960]{0,1:T(8,128)(2,1)} fusion(bf16[2048,960]{0,1:T(8,128)(2,1)} %bitcast.24, bf16[2048,1024]{1,0:T(8,128)(2,1)} %all-gather.5.cloned.1.call-done), kind=kOutput, calls=%fused_computation.6 | convolution fusion | flops 4027514880 | bytes 10092544 | tf_op jit(solution)/shard_map/dot_general | solution.py:10
  531.1 5.4 convert_bitcast_fusion
  536.5 61.5 %all-gather.11.cloned.1.call-done = bf16[2048,960]{0,1:T(8,128)(2,1)} async-done(((bf16[256,960]{0,1:T(8,128)(2,1)}), bf16[2048,960]{0,1:T(8,128)(2,1)}) %all-gather.11.cloned.1.call-update) | async-done | bytes 3932176 | tf_op jit(solution)/shard_map/all_gather | solution.py:58
  598.0 9.0 %convolution_convert_fusion.3 = bf16[960,1024]{1,0:T(8,128)(2,1)} fusion(bf16[2048,960]{0,1:T(8,128)(2,1)} %all-gather.11.cloned.1.call-done, bf16[2048,1024]{1,0:T(8,128)(2,1)} %all-gather.7.cloned.1.call-done), kind=kOutput, calls=%fused_computation.7 | convolution fusion | flops 4027514880 | bytes 10092544 | tf_op jit(solution)/shard_map/dot_general | solution.py:10
  607.0 77.1 %reduce-scatter.5.cloned.1.call-done = bf16[128,1024]{1,0:T(8,128)(2,1)} async-done(((bf16[2048,1024]{1,0:T(8,128)(2,1)}), bf16[128,1024]{1,0:T(8,128)(2,1)}) %reduce-scatter.5.cloned.1.call-update) | async-done | bytes 262160 | tf_op jit(solution)/shard_map/reduce_scatter | solution.py:67
  (20 shorter events, 0.1 us)
Async XLA Ops:
  7.2 70.3 %copy-start = (bf16[1024,960]{0,1:T(8,128)(2,1)S(1)}, bf16[1024,960]{0,1:T(8,128)(2,1)}, u32[]{:S(2)}) copy-start(bf16[1024,960]{0,1:T(8,128)(2,1)} %param.9) | copy-start | bytes 5898244
  7.2 61.2 %all-gather.5.cloned.1.call-start = ((), (), s32[]{:S(2)}) async-start(), calls=%async_computation.3 | async-start | bytes 4456448 | tf_op jit(solution)/shard_map/all_gather | solution.py:44
  7.9 116.7 %all-gather.7.cloned.1.call-start = ((), (), s32[]{:S(2)}) async-start(), calls=%async_computation.4 | async-start | bytes 4456448 | tf_op jit(solution)/shard_map/all_gather | solution.py:45
  10.5 372.4 %reduce-scatter.3.cloned.1.call-start = ((), (), s32[]{:S(2)}) async-start(), calls=%async_computation.5 | async-start | bytes 13271040 | tf_op jit(solution)/shard_map/reduce_scatter | solution.py:50
  68.4 9.1 %copy-start.5 = (bf16[2048,1024]{1,0:T(8,128)(2,1)S(1)}, bf16[2048,1024]{1,0:T(8,128)(2,1)}, u32[]{:S(2)}) copy-start(bf16[2048,1024]{1,0:T(8,128)(2,1)} %all-gather.5.cloned.1.call-done) | copy-start | bytes 12582916
  124.7 7.2 %copy-start.3 = (bf16[2048,960]{0,1:T(8,128)(2,1)S(1)}, bf16[2048,960]{0,1:T(8,128)(2,1)}, u32[]{:S(2)}) copy-start(bf16[2048,960]{0,1:T(8,128)(2,1)} %convolution_convert_fusion.1) | copy-start | bytes 11796484
  124.7 7.2 %copy-start.4 = (bf16[2048,960]{0,1:T(8,128)(2,1)S(1)}, bf16[2048,960]{0,1:T(8,128)(2,1)}, u32[]{:S(2)}) copy-start(bf16[2048,960]{0,1:T(8,128)(2,1)} %convolution_convert_fusion.2) | copy-start | bytes 11796484
  151.8 358.5 %all-gather.9.cloned.1.call-start = ((), (), s32[]{:S(2)}) async-start(), calls=%async_computation.6 | async-start | bytes 4423680 | tf_op jit(solution)/shard_map/all_gather | solution.py:62
  386.1 212.0 %all-gather.11.cloned.1.call-start = ((), (), s32[]{:S(2)}) async-start(), calls=%async_computation.8 | async-start | bytes 4423680 | tf_op jit(solution)/shard_map/all_gather | solution.py:58
  386.7 297.5 %reduce-scatter.5.cloned.1.call-start = ((), (), s32[]{:S(2)}) async-start(), calls=%async_computation.7 | async-start | bytes 4456448 | tf_op jit(solution)/shard_map/reduce_scatter | solution.py:67
  478.9 1.9 copy-start.2
  522.0 9.2 %copy-start.6 = (bf16[2048,1024]{1,0:T(8,128)(2,1)S(1)}, bf16[2048,1024]{1,0:T(8,128)(2,1)}, u32[]{:S(2)}) copy-start(bf16[2048,1024]{1,0:T(8,128)(2,1)} %all-gather.5.cloned.1.call-done) | copy-start | bytes 12582916
  522.0 9.1 %copy-start.7 = (bf16[2048,960]{0,1:T(8,128)(2,1)S(1)}, bf16[2048,960]{0,1:T(8,128)(2,1)}, u32[]{:S(2)}) copy-start(bf16[2048,960]{0,1:T(8,128)(2,1)} %all-gather.9.cloned.1.call-done) | copy-start | bytes 11796484
  598.0 86.1 %copy-start.1 = (bf16[1024,960]{0,1:T(8,128)(2,1)S(1)}, bf16[1024,960]{0,1:T(8,128)(2,1)}, u32[]{:S(2)}) copy-start(bf16[1024,960]{0,1:T(8,128)(2,1)} %param.9) | copy-start | bytes 5898244
Sparse Core Ops, SparseCore 0:
  10.5 57.8 all-gather.4
  71.5 53.1 all-gather.6
  151.9 230.9 reduce-scatter.2
  386.2 124.0 all-gather.8
  512.3 85.6 all-gather.10
  602.5 81.6 reduce-scatter.4
